TPU v7x, 32 devices: a whole 2x2x4 slice. The times are simulated.
32 devices in a mesh: dp: 2 (over core), cent: 16 (over z, y, x).
Axes of the slice: x: 2, y: 2, z: 4, core: 2. Of those that a mesh axis runs over, the one named last changes fastest.
Arguments:
- embeddings: bfloat16 [4096, 768], P(('dp', 'cent')), may hold values from -20 to 20
- fine_centroids: float32 [8192, 768], P('cent'), may hold values from -8 to 8
- parents: int32 [8192], P('cent'), may hold values from 0 to 2047
- coarse_centroids: float32 [2048, 768], P('cent'), may hold values from -6 to 6
Outputs:
- new_fine: float32 [8192, 768], P('cent')
- new_coarse: float32 [2048, 768], P('cent')
All inputs are finite; a program needn't handle non-finite values.
Results may differ from a plain program's by a relative error of at most 0.004.
Values may be sent and summed in bfloat16 or wider, within the bound.
A program may use at most 64 MiB of HBM per device.

v0:
```python
import math
import jax
import jax.numpy as jnp
from jax import lax
from jax.sharding import PartitionSpec as P

KC = 2048
sharpness = 0.1
coarse_prior = 16.0


def block_logits(one_block, narrow_centroids, half_norm):
    scores = lax.dot_general(
        one_block, narrow_centroids, (((1,), (1,)), ((), ())), preferred_element_type=jnp.float32
    )
    return sharpness * (scores - half_norm[None, :])


def coarse_terms(parent_ids, pooled, mass_rows):
    summed = jax.ops.segment_sum(pooled, parent_ids, num_segments=KC)
    weighted = jax.ops.segment_sum(mass_rows, parent_ids, num_segments=KC)
    return (summed, weighted)


def local(embeddings, fine_centroids, parents, coarse_centroids):
    gathered = lax.all_gather(embeddings, "cent", axis=0, tiled=True)
    row_count = gathered.shape[0]
    feat_width = gathered.shape[1]
    block_rows = math.gcd(row_count, 512)
    row_blocks = gathered.reshape(row_count // block_rows, block_rows, feat_width)
    narrow_centroids = fine_centroids.astype(jnp.bfloat16)
    half_norm = 0.5 * jnp.sum(fine_centroids * fine_centroids, axis=1)
    no_carry = jnp.zeros((), jnp.float32)

    def peak_step(carried, one_block):
        logits = block_logits(one_block, narrow_centroids, half_norm)
        return (carried, jnp.max(logits, axis=1))

    _, local_peak = lax.scan(peak_step, no_carry, row_blocks)
    row_peak = lax.pmax(local_peak.reshape(-1), "cent")

    def mass_step(carried, items):
        one_block, block_peak = items
        logits = block_logits(one_block, narrow_centroids, half_norm)
        return (carried, jnp.sum(jnp.exp(logits - block_peak[:, None]), axis=1))

    _, local_mass = lax.scan(mass_step, no_carry, (row_blocks, row_peak.reshape(-1, block_rows)))
    row_mass = lax.psum(local_mass.reshape(-1), "cent")

    def sum_step(carried, items):
        one_block, block_peak, block_mass = items
        logits = block_logits(one_block, narrow_centroids, half_norm)
        soft_weights = jnp.exp(logits - block_peak[:, None]) / block_mass[:, None]
        wide_block = one_block.astype(jnp.float32)
        summed = carried[0] + lax.dot_general(
            soft_weights,
            wide_block,
            (((0,), (0,)), ((), ())),
            precision=lax.Precision.HIGHEST,
            preferred_element_type=jnp.float32,
        )
        counted = carried[1] + jnp.sum(soft_weights, axis=0)
        return ((summed, counted), None)

    local_rows = fine_centroids.shape[0]
    start_state = (
        jnp.zeros(fine_centroids.shape, jnp.float32),
        jnp.zeros((local_rows,), jnp.float32),
    )
    stacked = (row_blocks, row_peak.reshape(-1, block_rows), row_mass.reshape(-1, block_rows))
    (fine_sums, fine_counts), _ = lax.scan(sum_step, start_state, stacked)
    total_sums, total_counts = lax.psum((fine_sums, fine_counts), "dp")
    pooled = fine_centroids + total_sums
    mass_rows = 1.0 + total_counts
    new_fine = pooled / mass_rows[:, None]
    col_width = feat_width // lax.axis_size("dp")
    first_col = lax.axis_index("dp") * col_width
    pooled_cols = lax.dynamic_slice_in_dim(pooled, first_col, col_width, 1)
    coarse_sum, coarse_mass = coarse_terms(parents, pooled_cols, mass_rows)
    owned_sum, owned_mass = (
        lax.psum_scatter(coarse_sum, "cent", scatter_dimension=0, tiled=True),
        lax.psum_scatter(coarse_mass, "cent", scatter_dimension=0, tiled=True),
    )
    old_cols = lax.dynamic_slice_in_dim(coarse_centroids, first_col, col_width, 1)
    new_cols = (coarse_prior * old_cols + owned_sum) / (coarse_prior + owned_mass)[:, None]
    new_coarse = lax.all_gather(new_cols, "dp", axis=1, tiled=True)
    return (new_fine, new_coarse)


def solution(mesh):
    in_specs = (P(("dp", "cent"), None), P("cent", None), P("cent"), P("cent", None))
    out_specs = (P("cent", None), P("cent", None))
    return jax.shard_map(local, mesh=mesh, in_specs=in_specs, out_specs=out_specs, check_vma=False)
```

profile of v0, /device:TPU:0, one launch (start us, length us, event | category | flops | bytes accessed | tf_op | source)
XLA Modules:
  0.0 365.4 jit_solution(11755867619514082077)
XLA Ops:
  7.2 0.7 all-gather.2.cloned.1.call-update
  7.9 0.0 all-reduce.3.cloned.1.call-start
  8.0 2.1 multiply_reduce_fusion
  10.1 71.3 %all-gather.2.cloned.1.call-done = bf16[2048,768]{1,0:T(8,128)(2,1)} async-done(((bf16[128,768]{1,0:T(8,128)(2,1)}), bf16[2048,768]{1,0:T(8,128)(2,1)}) %all-gather.2.cloned.1.call-update) | async-done | bytes 3145744 | tf_op jit(solution)/shard_map/all_gather | solution.py:26
  81.4 7.3 %while.33 = (s32[]{:T(128)}, f32[4,512]{1,0:T(4,128)S(1)}, bf16[4,512,768]{2,1,0:T(8,128)(2,1)}, bf16[512,768]{1,0:T(8,128)(2,1)S(1)}, f32[512]{0:T(512)S(1)}, /*index=5*/s32[]{:T(128)}, s32[]{:T(128)}) while((s32[]{:T(128)}, f32[4,512]{1,0:T(4,128)S(1)}, bf16[4,512,768]{2,1,0:T(8,128)(2,1)}, bf16[512,768]{1,0:T(8,128)(2,1)S(1)}, ...), condition=%wide.region_3.4_spmd, body=%wide.region_1.3_spmd.sunk | while | flops 403439104 | bytes 1581649 | solution.py:39
  81.4 1.7 fusion.44
  83.1 0.1 dynamic_update_slice.9
  83.2 1.8 fusion.44
  85.0 0.1 dynamic_update_slice.9
  85.0 1.8 fusion.44
  86.8 0.1 dynamic_update_slice.9
  86.8 1.8 fusion.44
  88.6 0.1 dynamic_update_slice.9
  88.7 39.8 %pmax.7 = f32[4,512]{1,0:T(4,128)S(1)} all-reduce(f32[4,512]{1,0:T(4,128)S(1)} %get-tuple-element.104), channel_id=1, replica_groups=mesh['dp'=2,'cent'=16] {'cent'}, use_global_device_ids=true, to_apply=%region_4.5 | all-reduce | flops 2048 | bytes 16384 | tf_op jit(solution)/shard_map/pmax | solution.py:40
  128.5 7.7 %while.34 = (s32[]{:T(128)}, f32[4,512]{1,0:T(4,128)S(1)}, bf16[4,512,768]{2,1,0:T(8,128)(2,1)}, bf16[512,768]{1,0:T(8,128)(2,1)S(1)}, f32[512]{0:T(512)S(1)}, /*index=5*/f32[4,512]{1,0:T(4,128)S(1)}, s32[]{:T(128)}, s32[]{:T(128)}) while((s32[]{:T(128)}, f32[4,512]{1,0:T(4,128)S(1)}, bf16[4,512,768]{2,1,0:T(8,128)(2,1)}, ...), condition=%wide.region_7.8_spmd, body=%wide.region_5.7_spmd.sunk | while | flops 403701248 | bytes 1587805 | solution.py:47
  128.5 1.8 fusion.47
  130.4 0.1 dynamic_update_slice.10
  130.5 1.8 fusion.47
  132.3 0.1 dynamic_update_slice.10
  132.4 1.8 fusion.47
  134.2 0.1 dynamic_update_slice.10
  134.3 1.8 fusion.47
  136.1 0.1 dynamic_update_slice.10
  136.2 37.1 %psum.21 = f32[4,512]{1,0:T(4,128)S(1)} all-reduce(f32[4,512]{1,0:T(4,128)S(1)} %get-tuple-element.105), channel_id=1, replica_groups=mesh['dp'=2,'cent'=16] {'cent'}, use_global_device_ids=true, to_apply=%region_8.9 | all-reduce | flops 2048 | bytes 16384 | tf_op jit(solution)/shard_map/psum | solution.py:48
  173.3 20.2 %while.35 = (s32[]{:T(128)}, f32[512,768]{1,0:T(8,128)S(1)}, f32[512]{0:T(512)S(1)}, bf16[4,512,768]{2,1,0:T(8,128)(2,1)}, bf16[512,768]{1,0:T(8,128)(2,1)S(1)},...) while((s32[]{:T(128)}, f32[512,768]{1,0:T(8,128)S(1)}, ...), condition=%wide.region_11.12_spmd.clone, body=%wide.region_9.11_spmd.clone.sunk | while | flops 2820669952 | bytes 7625844 | solution.py:71
  173.4 1.9 fusion.51
  175.2 3.1 select_add_fusion.4
  178.4 1.9 fusion.51
  180.3 3.1 select_add_fusion.4
  183.5 1.9 fusion.51
  185.4 3.1 select_add_fusion.4
  188.6 1.9 fusion.51
  190.4 3.1 select_add_fusion.4
  193.6 1.1 copy-done
  194.8 0.0 reduce-scatter.2.cloned.1.call-start
  194.8 2.5 psum.23
  197.3 15.7 %all-reduce.3.cloned.1.call-done = f32[512,768]{1,0:T(8,128)} async-done(((f32[512,768]{1,0:T(8,128)}), f32[512,768]{1,0:T(8,128)}) %all-reduce.3.cloned.1.call-update) | async-done | bytes 1572880 | tf_op jit(solution)/shard_map/psum | solution.py:72
  213.0 2.8 broadcast_divide_fusion
  215.8 5.6 %scatter_custom_fusion = f32[2048,384]{1,0:T(8,128)} fusion(s32[512]{0:T(512)} %param.12, f32[]{:T(128)} %constant.35.clone.1, f32[512,768]{1,0:T(8,128)S(1)} %get-tuple-element.174, s32[]{:T(128)} %constant.39.clone.1, s32[]{:T(128)S(6)} %select_n.4), kind=kCustom, calls=%fused_computation.32 | custom fusion | flops 196608 | bytes 3933188 | tf_op jit(solution)/shard_map/scatter-add | solution.py:20
  221.4 0.6 copy-done.3
  222.0 0.6 dynamic-slice
  223.3 3.4 scatter_custom_fusion.1
  226.7 42.6 %all-reduce = f32[2048]{0:T(1024)S(1)} all-reduce(f32[2048]{0:T(1024)S(1)} %scatter_custom_fusion.1), channel_id=3, replica_groups=mesh['dp'=2,'cent'=16] {'cent'}, use_global_device_ids=true, to_apply=%region_17.18.clone | all-reduce | flops 2048 | bytes 16384
  269.3 0.1 dynamic-slice_add_fusion
  269.4 85.6 %reduce-scatter.2.cloned.1.call-done = f32[128,384]{1,0:T(8,128)} async-done(((f32[2048,384]{1,0:T(8,128)}), f32[128,384]{1,0:T(8,128)}) %reduce-scatter.2.cloned.1.call-update) | async-done | bytes 196624 | tf_op jit(solution)/shard_map/reduce_scatter | solution.py:81
  355.0 1.0 add_divide_fusion
  356.0 2.1 all_gather.7
  358.1 0.7 copy.33
  (27 shorter events, 0.2 us)
Async XLA Ops:
  7.2 74.2 %all-gather.2.cloned.1.call-start = ((), (), s32[]{:S(2)}) async-start(), calls=%async_computation.1 | async-start | bytes 3342336 | tf_op jit(solution)/shard_map/all_gather | solution.py:26
  7.9 205.1 %all-reduce.3.cloned.1.call-start = ((), (), s32[]{:S(2)}) async-start(), calls=%async_computation.2 | async-start | bytes 3145728 | tf_op jit(solution)/shard_map/psum | solution.py:72
  193.6 1.1 copy-start
  193.6 19.4 %copy-start.1 = (f32[512,768]{1,0:T(8,128)S(1)}, f32[512,768]{1,0:T(8,128)}, u32[]{:S(2)}) copy-start(f32[512,768]{1,0:T(8,128)} %param.11) | copy-start | bytes 4718596
  194.8 160.3 %reduce-scatter.2.cloned.1.call-start = ((), (), s32[]{:S(2)}) async-start(), calls=%async_computation.3 | async-start | bytes 3342336 | tf_op jit(solution)/shard_map/reduce_scatter | solution.py:81
  221.4 0.7 copy-start.3
  221.4 133.6 %copy-start.2 = (f32[128,768]{1,0:T(8,128)S(1)}, f32[128,768]{1,0:T(8,128)}, u32[]{:S(2)}) copy-start(f32[128,768]{1,0:T(8,128)} %param.13) | copy-start | bytes 1179652
Sparse Core Ops, SparseCore 0:
  10.7 70.5 all-gather.1
  194.9 18.0 all-reduce.2
  221.5 133.4 reduce-scatter.1
where the time goes:
time: 366 us; the launch traced here: 365 us
  waiting for transfers between devices  173 us (47%)
  blocking collectives  124 us (34%)
  matrix products  34.3 us (9%)
  other arithmetic  15.1 us (4%)
  between operations  14.5 us (4%)
    reduce_scatter x1, waiting for transfers between devices, local(): lax.psum_scatter(coarse_sum, 'cent', scatter_dimension=0, tiled=True)  85.6 us
    all_gather x1, waiting for transfers between devices, local(): gathered = lax.all_gather(embeddings, 'cent', axis=0, tiled=True)  71.3 us
    unnamed x1, blocking collectives  42.6 us
    pmax x1, blocking collectives, local(): row_peak = lax.pmax(local_peak.reshape(-1), 'cent')  39.8 us
    psum x1, blocking collectives, local(): row_mass = lax.psum(local_mass.reshape(-1), 'cent')  37.1 us
    dot_general x12, matrix products, block_logits(): lax.dot_general(one_block, narrow_centroids, (((1,), (1,)), ((), ())), pr...  21.8 us
    psum x1, waiting for transfers between devices, local(): total_sums, total_counts = lax.psum((fine_sums, fine_counts), 'dp')  15.7 us
    dot_general x4, matrix products, sum_step(): lax.dot_general(soft_weights, wide_block, (((0,), (0,)), ((), ())), preci...  12.5 us
  transfers between devices with their start and end apart: 3, of which 3 were waited for; matrix products, arithmetic and copies ran while one was open for 2% of the time, Pallas kernels for 0%

commit v1 on v0

--- a/solution.py
+++ b/solution.py
@@ -23,7 +23,13 @@
 
 
 def local(embeddings, fine_centroids, parents, coarse_centroids):
-    gathered = lax.all_gather(embeddings, "cent", axis=0, tiled=True)
+    devices = lax.axis_size("cent")
+    held, shards = (embeddings, [embeddings])
+    for _ in range(devices - 1):
+        held = lax.ppermute(held, "cent", [(i, (i + 1) % devices) for i in range(devices)])
+        shards.insert(0, held)
+    row_of_blocks = jnp.concatenate(shards, axis=0)
+    gathered = jnp.roll(row_of_blocks, (lax.axis_index("cent") + 1) * embeddings.shape[0], axis=0)
     row_count = gathered.shape[0]
     feat_width = gathered.shape[1]
     block_rows = math.gcd(row_count, 512)

time: 366 us -> 451 us (1.23)
  waiting for transfers between devices: 173 us -> 242 us
  local copies, waits for them, and re-layouts: 3.56 us -> 12.2 us
    ppermute x0 -> x15, waiting for transfers between devices: none -> 142 us  [local(): lax.ppermute(held, 'cent', [(i, (i + 1) % devices) for i in range(devices)])]
    all_gather x1 -> x0, waiting for transfers between devices: 71.3 us -> none  [local(): gathered = lax.all_gather(embeddings, 'cent', axis=0, tiled=True)]
    unnamed x10 -> x49, local copies, waits for them, and re-layouts: 3.09 us -> 9.87 us
  transfers between devices with their start and end apart: 3 -> 17, of which waited for: 3 -> 17; matrix products, arithmetic and copies ran while one was open for 2% -> 2% of each run, Pallas kernels for 0% -> 0%
where the time goes in v1:
time: 451 us; the launch traced here: 450 us
  waiting for transfers between devices  242 us (54%)
  blocking collectives  123 us (27%)
  matrix products  37.2 us (8%)
  other arithmetic  16.4 us (4%)
  between operations  15.1 us (3%)
  local copies, waits for them, and re-layouts  12.2 us (3%)
    ppermute x15, waiting for transfers between devices, local(): lax.ppermute(held, 'cent', [(i, (i + 1) % devices) for i in range(devices)])  142 us
    reduce_scatter x1, waiting for transfers between devices, local(): lax.psum_scatter(coarse_sum, 'cent', scatter_dimension=0, tiled=True)  86.2 us
    unnamed x1, blocking collectives  42.8 us
    psum x1, blocking collectives, local(): row_mass = lax.psum(local_mass.reshape(-1), 'cent')  39.1 us
    pmax x1, blocking collectives, local(): row_peak = lax.pmax(local_peak.reshape(-1), 'cent')  37.1 us
    dot_general x12, matrix products, block_logits(): lax.dot_general(one_block, narrow_centroids, (((1,), (1,)), ((), ())), pr...  24.7 us
    psum x1, waiting for transfers between devices, local(): total_sums, total_counts = lax.psum((fine_sums, fine_counts), 'dp')  13.8 us
    dot_general x4, matrix products, sum_step(): lax.dot_general(soft_weights, wide_block, (((0,), (0,)), ((), ())), preci...  12.5 us
  transfers between devices with their start and end apart: 17, of which 17 were waited for; matrix products, arithmetic and copies ran while one was open for 2% of the time, Pallas kernels for 0%

profile of v1, /device:TPU:0, one launch (start us, length us, event | category | flops | bytes accessed | tf_op | source)
XLA Modules:
  0.0 449.7 jit_solution(14679435636124609121)
XLA Ops:
  7.2 3.0 collective-permute-start
  10.2 9.1 %collective-permute-done = bf16[128,768]{1,0:T(8,128)(2,1)S(1)} collective-permute-done((bf16[128,768]{1,0:T(8,128)(2,1)}, bf16[128,768]{1,0:T(8,128)(2,1)S(1)}, u32[]{:S(2)}, u32[]{:S(2)}) %collective-permute-start) | collective-permute-done | bytes 196640 | tf_op jit(solution)/shard_map/ppermute | solution.py:29
  19.3 9.7 %collective-permute-done.1 = bf16[128,768]{1,0:T(8,128)(2,1)S(1)} collective-permute-done((bf16[128,768]{1,0:T(8,128)(2,1)S(1)}, bf16[128,768]{1,0:T(8,128)(2,1)S(1)}, u32[]{:S(2)}, u32[]{:S(2)}) %collective-permute-start.1) | collective-permute-done | bytes 196640 | tf_op jit(solution)/shard_map/ppermute | solution.py:29
  29.0 9.3 %collective-permute-done.2 = bf16[128,768]{1,0:T(8,128)(2,1)S(1)} collective-permute-done((bf16[128,768]{1,0:T(8,128)(2,1)S(1)}, bf16[128,768]{1,0:T(8,128)(2,1)S(1)}, u32[]{:S(2)}, u32[]{:S(2)}) %collective-permute-start.2) | collective-permute-done | bytes 196640 | tf_op jit(solution)/shard_map/ppermute | solution.py:29
  38.3 9.3 %collective-permute-done.3 = bf16[128,768]{1,0:T(8,128)(2,1)S(1)} collective-permute-done((bf16[128,768]{1,0:T(8,128)(2,1)S(1)}, bf16[128,768]{1,0:T(8,128)(2,1)S(1)}, u32[]{:S(2)}, u32[]{:S(2)}) %collective-permute-start.3) | collective-permute-done | bytes 196640 | tf_op jit(solution)/shard_map/ppermute | solution.py:29
  47.5 9.3 %collective-permute-done.4 = bf16[128,768]{1,0:T(8,128)(2,1)S(1)} collective-permute-done((bf16[128,768]{1,0:T(8,128)(2,1)S(1)}, bf16[128,768]{1,0:T(8,128)(2,1)S(1)}, u32[]{:S(2)}, u32[]{:S(2)}) %collective-permute-start.4) | collective-permute-done | bytes 196640 | tf_op jit(solution)/shard_map/ppermute | solution.py:29
  56.8 9.3 %collective-permute-done.5 = bf16[128,768]{1,0:T(8,128)(2,1)S(1)} collective-permute-done((bf16[128,768]{1,0:T(8,128)(2,1)S(1)}, bf16[128,768]{1,0:T(8,128)(2,1)S(1)}, u32[]{:S(2)}, u32[]{:S(2)}) %collective-permute-start.5) | collective-permute-done | bytes 196640 | tf_op jit(solution)/shard_map/ppermute | solution.py:29
  66.1 10.4 %collective-permute-done.6 = bf16[128,768]{1,0:T(8,128)(2,1)S(1)} collective-permute-done((bf16[128,768]{1,0:T(8,128)(2,1)S(1)}, bf16[128,768]{1,0:T(8,128)(2,1)S(1)}, u32[]{:S(2)}, u32[]{:S(2)}) %collective-permute-start.6) | collective-permute-done | bytes 196640 | tf_op jit(solution)/shard_map/ppermute | solution.py:29
  76.5 11.2 %collective-permute-done.7 = bf16[128,768]{1,0:T(8,128)(2,1)S(1)} collective-permute-done((bf16[128,768]{1,0:T(8,128)(2,1)S(1)}, bf16[128,768]{1,0:T(8,128)(2,1)S(1)}, u32[]{:S(2)}, u32[]{:S(2)}) %collective-permute-start.7) | collective-permute-done | bytes 196640 | tf_op jit(solution)/shard_map/ppermute | solution.py:29
  87.7 10.3 %collective-permute-done.8 = bf16[128,768]{1,0:T(8,128)(2,1)S(1)} collective-permute-done((bf16[128,768]{1,0:T(8,128)(2,1)S(1)}, bf16[128,768]{1,0:T(8,128)(2,1)S(1)}, u32[]{:S(2)}, u32[]{:S(2)}) %collective-permute-start.8) | collective-permute-done | bytes 196640 | tf_op jit(solution)/shard_map/ppermute | solution.py:29
  98.0 10.1 %collective-permute-done.9 = bf16[128,768]{1,0:T(8,128)(2,1)S(1)} collective-permute-done((bf16[128,768]{1,0:T(8,128)(2,1)S(1)}, bf16[128,768]{1,0:T(8,128)(2,1)S(1)}, u32[]{:S(2)}, u32[]{:S(2)}) %collective-permute-start.9) | collective-permute-done | bytes 196640 | tf_op jit(solution)/shard_map/ppermute | solution.py:29
  108.8 9.3 %collective-permute-done.10 = bf16[128,768]{1,0:T(8,128)(2,1)S(1)} collective-permute-done((bf16[128,768]{1,0:T(8,128)(2,1)S(1)}, bf16[128,768]{1,0:T(8,128)(2,1)S(1)}, u32[]{:S(2)}, u32[]{:S(2)}) %collective-permute-start.10) | collective-permute-done | bytes 196640 | tf_op jit(solution)/shard_map/ppermute | solution.py:29
  118.8 9.4 %collective-permute-done.11 = bf16[128,768]{1,0:T(8,128)(2,1)} collective-permute-done((bf16[128,768]{1,0:T(8,128)(2,1)S(1)}, bf16[128,768]{1,0:T(8,128)(2,1)}, u32[]{:S(2)}, u32[]{:S(2)}) %collective-permute-start.11) | collective-permute-done | bytes 196640 | tf_op jit(solution)/shard_map/ppermute | solution.py:29
  128.2 9.6 %collective-permute-done.12 = bf16[128,768]{1,0:T(8,128)(2,1)} collective-permute-done((bf16[128,768]{1,0:T(8,128)(2,1)}, bf16[128,768]{1,0:T(8,128)(2,1)}, u32[]{:S(2)}, u32[]{:S(2)}) %collective-permute-start.12) | collective-permute-done | bytes 196640 | tf_op jit(solution)/shard_map/ppermute | solution.py:29
  137.7 2.9 multiply_reduce_fusion
  140.7 6.5 %collective-permute-done.13 = bf16[128,768]{1,0:T(8,128)(2,1)S(1)} collective-permute-done((bf16[128,768]{1,0:T(8,128)(2,1)}, bf16[128,768]{1,0:T(8,128)(2,1)S(1)}, u32[]{:S(2)}, u32[]{:S(2)}) %collective-permute-start.13) | collective-permute-done | bytes 196640 | tf_op jit(solution)/shard_map/ppermute | solution.py:29
  147.2 9.3 %collective-permute-done.14 = bf16[128,768]{1,0:T(8,128)(2,1)S(1)} collective-permute-done((bf16[128,768]{1,0:T(8,128)(2,1)S(1)}, bf16[128,768]{1,0:T(8,128)(2,1)S(1)}, u32[]{:S(2)}, u32[]{:S(2)}) %collective-permute-start.14) | collective-permute-done | bytes 196640 | tf_op jit(solution)/shard_map/ppermute | solution.py:29
  162.8 1.9 constant_dynamic-slice_fusion.3
  164.6 8.2 %while.33 = (s32[]{:T(128)}, f32[4,512]{1,0:T(4,128)S(1)}, bf16[4,512,768]{2,1,0:T(8,128)(2,1)}, bf16[512,768]{1,0:T(8,128)(2,1)}, f32[512]{0:T(512)S(1)}, /*index=5*/s32[]{:T(128)}, s32[]{:T(128)}) while((s32[]{:T(128)}, f32[4,512]{1,0:T(4,128)S(1)}, bf16[4,512,768]{2,1,0:T(8,128)(2,1)}, bf16[512,768]{1,0:T(8,128)(2,1)}, f32[512]{0:T(512)S(1)}, ...), condition=%wide.region_3.4_spmd, body=%wide.region_1.3_spmd.sunk | while | flops 403439104 | bytes 1581649 | solution.py:45
  164.6 2.0 fusion.44
  166.7 2.0 fusion.44
  168.8 2.0 fusion.44
  170.8 2.0 fusion.44
  172.9 37.1 %pmax.7 = f32[4,512]{1,0:T(4,128)S(1)} all-reduce(f32[4,512]{1,0:T(4,128)S(1)} %get-tuple-element.104), channel_id=1, replica_groups=mesh['dp'=2,'cent'=16] {'cent'}, use_global_device_ids=true, to_apply=%region_4.5 | all-reduce | flops 2048 | bytes 16384 | tf_op jit(solution)/shard_map/pmax | solution.py:46
  210.0 8.6 %while.34 = (s32[]{:T(128)}, f32[4,512]{1,0:T(4,128)S(1)}, bf16[4,512,768]{2,1,0:T(8,128)(2,1)}, bf16[512,768]{1,0:T(8,128)(2,1)}, f32[512]{0:T(512)S(1)}, /*index=5*/f32[4,512]{1,0:T(4,128)S(1)}, s32[]{:T(128)}, s32[]{:T(128)}) while((s32[]{:T(128)}, f32[4,512]{1,0:T(4,128)S(1)}, bf16[4,512,768]{2,1,0:T(8,128)(2,1)}, ...), condition=%wide.region_7.8_spmd, body=%wide.region_5.7_spmd.sunk | while | flops 403701248 | bytes 1587805 | solution.py:53
  210.0 2.1 fusion.47
  212.2 2.1 fusion.47
  214.3 2.1 fusion.47
  216.5 2.1 fusion.47
  218.6 39.1 %psum.21 = f32[4,512]{1,0:T(4,128)S(1)} all-reduce(f32[4,512]{1,0:T(4,128)S(1)} %get-tuple-element.105), channel_id=1, replica_groups=mesh['dp'=2,'cent'=16] {'cent'}, use_global_device_ids=true, to_apply=%region_8.9 | all-reduce | flops 2048 | bytes 16384 | tf_op jit(solution)/shard_map/psum | solution.py:54
  257.7 21.2 %while.35 = (s32[]{:T(128)}, f32[512,768]{1,0:T(8,128)S(1)}, f32[512]{0:T(512)S(1)}, bf16[4,512,768]{2,1,0:T(8,128)(2,1)}, bf16[512,768]{1,0:T(8,128)(2,1)}, /*i...) while((s32[]{:T(128)}, f32[512,768]{1,0:T(8,128)S(1)}, ...), condition=%wide.region_11.12_spmd.clone, body=%wide.region_9.11_spmd.clone.sunk | while | flops 2820669952 | bytes 7625844 | solution.py:77
  257.7 2.1 fusion.51
  259.8 3.1 select_add_fusion.4
  263.0 2.1 fusion.51
  265.1 3.1 select_add_fusion.4
  268.3 2.1 fusion.51
  270.4 3.1 select_add_fusion.4
  273.6 2.1 fusion.51
  275.7 3.1 select_add_fusion.4
  278.9 1.1 copy-done
  280.1 2.5 psum.23
  282.6 13.8 %all-reduce.3.cloned.1.call-done = f32[512,768]{1,0:T(8,128)} async-done(((f32[512,768]{1,0:T(8,128)}), f32[512,768]{1,0:T(8,128)}) %all-reduce.3.cloned.1.call-update) | async-done | bytes 1572880 | tf_op jit(solution)/shard_map/psum | solution.py:78
  296.4 3.3 broadcast_divide_fusion
  299.7 5.6 %scatter_custom_fusion = f32[2048,384]{1,0:T(8,128)} fusion(s32[512]{0:T(512)} %param.12, f32[]{:T(128)} %constant.78.clone.1, f32[512,768]{1,0:T(8,128)S(1)} %get-tuple-element.174, s32[]{:T(128)} %constant.77.clone.1, s32[]{:T(128)S(6)} %select_n.19), kind=kCustom, calls=%fused_computation.32 | custom fusion | flops 196608 | bytes 3933188 | tf_op jit(solution)/shard_map/scatter-add | solution.py:20
  306.6 3.4 scatter_custom_fusion.1
  310.0 42.8 %all-reduce = f32[2048]{0:T(1024)S(1)} all-reduce(f32[2048]{0:T(1024)S(1)} %scatter_custom_fusion.1), channel_id=3, replica_groups=mesh['dp'=2,'cent'=16] {'cent'}, use_global_device_ids=true, to_apply=%region_17.18.clone | all-reduce | flops 2048 | bytes 16384
  352.8 86.2 %reduce-scatter.2.cloned.1.call-done = f32[128,384]{1,0:T(8,128)} async-done(((f32[2048,384]{1,0:T(8,128)}), f32[128,384]{1,0:T(8,128)}) %reduce-scatter.2.cloned.1.call-update) | async-done | bytes 196624 | tf_op jit(solution)/shard_map/reduce_scatter | solution.py:87
  440.1 2.1 all_gather.3
  (95 shorter events, 10.5 us)
Async XLA Ops:
  7.2 153.3 %copy-start.1 = (bf16[128,768]{1,0:T(8,128)(2,1)S(1)}, bf16[128,768]{1,0:T(8,128)(2,1)}, u32[]{:S(2)}) copy-start(bf16[128,768]{1,0:T(8,128)(2,1)} %param.10) | copy-start | bytes 589828
  7.2 289.3 %all-reduce.3.cloned.1.call-start = ((), (), s32[]{:S(2)}) async-start(), calls=%async_computation.1 | async-start | bytes 3145728 | tf_op jit(solution)/shard_map/psum | solution.py:78
  7.2 12.1 %collective-permute-start = (bf16[128,768]{1,0:T(8,128)(2,1)}, bf16[128,768]{1,0:T(8,128)(2,1)S(1)}, u32[]{:S(2)}, u32[]{:S(2)}) collective-permute-start(bf16[128,768]{1,0:T(8,128)(2,1)} %param.10), channel_id=1, source_target_pairs={{0,1},{1,2},{2,3},{3,4},{4,5},{5,6},{6,7},{7,8},{8,9},{9,10},{10,1... | collective-permute-start | bytes 589832 | tf_op jit(solution)/shard_map/ppermute | solution.py:29
  19.3 9.7 %collective-permute-start.1 = (bf16[128,768]{1,0:T(8,128)(2,1)S(1)}, bf16[128,768]{1,0:T(8,128)(2,1)S(1)}, u32[]{:S(2)}, u32[]{:S(2)}) collective-permute-start(bf16[128,768]{1,0:T(8,128)(2,1)S(1)} %collective-permute-done), channel_id=1, source_target_pairs={{0,1},{1,2},{2,3},{3,4},{4,5},{5,6},{6,7},{7,8},{8,9},{9,10},{10,1... | collective-permute-start | bytes 589832 | tf_op jit(solution)/shard_map/ppermute | solution.py:29
  29.0 9.3 %collective-permute-start.2 = (bf16[128,768]{1,0:T(8,128)(2,1)S(1)}, bf16[128,768]{1,0:T(8,128)(2,1)S(1)}, u32[]{:S(2)}, u32[]{:S(2)}) collective-permute-start(bf16[128,768]{1,0:T(8,128)(2,1)S(1)} %collective-permute-done.1), channel_id=1, source_target_pairs={{0,1},{1,2},{2,3},{3,4},{4,5},{5,6},{6,7},{7,8},{8,9},{9,10},{10,1... | collective-permute-start | bytes 589832 | tf_op jit(solution)/shard_map/ppermute | solution.py:29
  38.3 9.3 %collective-permute-start.3 = (bf16[128,768]{1,0:T(8,128)(2,1)S(1)}, bf16[128,768]{1,0:T(8,128)(2,1)S(1)}, u32[]{:S(2)}, u32[]{:S(2)}) collective-permute-start(bf16[128,768]{1,0:T(8,128)(2,1)S(1)} %collective-permute-done.2), channel_id=1, source_target_pairs={{0,1},{1,2},{2,3},{3,4},{4,5},{5,6},{6,7},{7,8},{8,9},{9,10},{10,1... | collective-permute-start | bytes 589832 | tf_op jit(solution)/shard_map/ppermute | solution.py:29
  47.5 9.3 %collective-permute-start.4 = (bf16[128,768]{1,0:T(8,128)(2,1)S(1)}, bf16[128,768]{1,0:T(8,128)(2,1)S(1)}, u32[]{:S(2)}, u32[]{:S(2)}) collective-permute-start(bf16[128,768]{1,0:T(8,128)(2,1)S(1)} %collective-permute-done.3), channel_id=1, source_target_pairs={{0,1},{1,2},{2,3},{3,4},{4,5},{5,6},{6,7},{7,8},{8,9},{9,10},{10,1... | collective-permute-start | bytes 589832 | tf_op jit(solution)/shard_map/ppermute | solution.py:29
  56.8 9.3 %collective-permute-start.5 = (bf16[128,768]{1,0:T(8,128)(2,1)S(1)}, bf16[128,768]{1,0:T(8,128)(2,1)S(1)}, u32[]{:S(2)}, u32[]{:S(2)}) collective-permute-start(bf16[128,768]{1,0:T(8,128)(2,1)S(1)} %collective-permute-done.4), channel_id=1, source_target_pairs={{0,1},{1,2},{2,3},{3,4},{4,5},{5,6},{6,7},{7,8},{8,9},{9,10},{10,1... | collective-permute-start | bytes 589832 | tf_op jit(solution)/shard_map/ppermute | solution.py:29
  66.1 10.4 %collective-permute-start.6 = (bf16[128,768]{1,0:T(8,128)(2,1)S(1)}, bf16[128,768]{1,0:T(8,128)(2,1)S(1)}, u32[]{:S(2)}, u32[]{:S(2)}) collective-permute-start(bf16[128,768]{1,0:T(8,128)(2,1)S(1)} %collective-permute-done.5), channel_id=1, source_target_pairs={{0,1},{1,2},{2,3},{3,4},{4,5},{5,6},{6,7},{7,8},{8,9},{9,10},{10,1... | collective-permute-start | bytes 589832 | tf_op jit(solution)/shard_map/ppermute | solution.py:29
  76.5 11.2 %collective-permute-start.7 = (bf16[128,768]{1,0:T(8,128)(2,1)S(1)}, bf16[128,768]{1,0:T(8,128)(2,1)S(1)}, u32[]{:S(2)}, u32[]{:S(2)}) collective-permute-start(bf16[128,768]{1,0:T(8,128)(2,1)S(1)} %collective-permute-done.6), channel_id=1, source_target_pairs={{0,1},{1,2},{2,3},{3,4},{4,5},{5,6},{6,7},{7,8},{8,9},{9,10},{10,1... | collective-permute-start | bytes 589832 | tf_op jit(solution)/shard_map/ppermute | solution.py:29
  87.7 10.3 %collective-permute-start.8 = (bf16[128,768]{1,0:T(8,128)(2,1)S(1)}, bf16[128,768]{1,0:T(8,128)(2,1)S(1)}, u32[]{:S(2)}, u32[]{:S(2)}) collective-permute-start(bf16[128,768]{1,0:T(8,128)(2,1)S(1)} %collective-permute-done.7), channel_id=1, source_target_pairs={{0,1},{1,2},{2,3},{3,4},{4,5},{5,6},{6,7},{7,8},{8,9},{9,10},{10,1... | collective-permute-start | bytes 589832 | tf_op jit(solution)/shard_map/ppermute | solution.py:29
  98.0 10.1 %collective-permute-start.9 = (bf16[128,768]{1,0:T(8,128)(2,1)S(1)}, bf16[128,768]{1,0:T(8,128)(2,1)S(1)}, u32[]{:S(2)}, u32[]{:S(2)}) collective-permute-start(bf16[128,768]{1,0:T(8,128)(2,1)S(1)} %collective-permute-done.8), channel_id=1, source_target_pairs={{0,1},{1,2},{2,3},{3,4},{4,5},{5,6},{6,7},{7,8},{8,9},{9,10},{10,1... | collective-permute-start | bytes 589832 | tf_op jit(solution)/shard_map/ppermute | solution.py:29
  108.1 0.7 copy-start.2
  108.8 9.3 %collective-permute-start.10 = (bf16[128,768]{1,0:T(8,128)(2,1)S(1)}, bf16[128,768]{1,0:T(8,128)(2,1)S(1)}, u32[]{:S(2)}, u32[]{:S(2)}) collective-permute-start(bf16[128,768]{1,0:T(8,128)(2,1)S(1)} %collective-permute-done.9), channel_id=1, source_target_pairs={{0,1},{1,2},{2,3},{3,4},{4,5},{5,6},{6,7},{7,8},{8,9},{9,10},{10,1... | collective-permute-start | bytes 589832 | tf_op jit(solution)/shard_map/ppermute | solution.py:29
  118.1 0.7 copy-start.4
  118.8 9.4 %collective-permute-start.11 = (bf16[128,768]{1,0:T(8,128)(2,1)S(1)}, bf16[128,768]{1,0:T(8,128)(2,1)}, u32[]{:S(2)}, u32[]{:S(2)}) collective-permute-start(bf16[128,768]{1,0:T(8,128)(2,1)S(1)} %collective-permute-done.10), channel_id=1, source_target_pairs={{0,1},{1,2},{2,3},{3,4},{4,5},{5,6},{6,7},{7,8},{8,9},{9,10},{10,1... | collective-permute-start | bytes 589832 | tf_op jit(solution)/shard_map/ppermute | solution.py:29
  128.1 9.6 %collective-permute-start.12 = (bf16[128,768]{1,0:T(8,128)(2,1)}, bf16[128,768]{1,0:T(8,128)(2,1)}, u32[]{:S(2)}, u32[]{:S(2)}) collective-permute-start(bf16[128,768]{1,0:T(8,128)(2,1)} %collective-permute-done.11), channel_id=1, source_target_pairs={{0,1},{1,2},{2,3},{3,4},{4,5},{5,6},{6,7},{7,8},{8,9},{9,10},{10,1... | collective-permute-start | bytes 589832 | tf_op jit(solution)/shard_map/ppermute | solution.py:29
  128.2 34.3 %copy-start.5 = (bf16[128,768]{1,0:T(8,128)(2,1)S(1)}, bf16[128,768]{1,0:T(8,128)(2,1)}, u32[]{:S(2)}) copy-start(bf16[128,768]{1,0:T(8,128)(2,1)} %copy-done.4) | copy-start | bytes 589828
  128.2 34.4 %copy-start.3 = (bf16[128,768]{1,0:T(8,128)(2,1)S(1)}, bf16[128,768]{1,0:T(8,128)(2,1)}, u32[]{:S(2)}) copy-start(bf16[128,768]{1,0:T(8,128)(2,1)} %copy-done.2) | copy-start | bytes 589828
  137.7 9.5 %collective-permute-start.13 = (bf16[128,768]{1,0:T(8,128)(2,1)}, bf16[128,768]{1,0:T(8,128)(2,1)S(1)}, u32[]{:S(2)}, u32[]{:S(2)}) collective-permute-start(bf16[128,768]{1,0:T(8,128)(2,1)} %collective-permute-done.12), channel_id=1, source_target_pairs={{0,1},{1,2},{2,3},{3,4},{4,5},{5,6},{6,7},{7,8},{8,9},{9,10},{10,1... | collective-permute-start | bytes 589832 | tf_op jit(solution)/shard_map/ppermute | solution.py:29
  147.2 9.3 %collective-permute-start.14 = (bf16[128,768]{1,0:T(8,128)(2,1)S(1)}, bf16[128,768]{1,0:T(8,128)(2,1)S(1)}, u32[]{:S(2)}, u32[]{:S(2)}) collective-permute-start(bf16[128,768]{1,0:T(8,128)(2,1)S(1)} %collective-permute-done.13), channel_id=1, source_target_pairs={{0,1},{1,2},{2,3},{3,4},{4,5},{5,6},{6,7},{7,8},{8,9},{9,10},{10,1... | collective-permute-start | bytes 589832 | tf_op jit(solution)/shard_map/ppermute | solution.py:29
  278.9 1.1 copy-start
  280.1 159.0 %reduce-scatter.2.cloned.1.call-start = ((), (), s32[]{:S(2)}) async-start(), calls=%async_computation.2 | async-start | bytes 3342336 | tf_op jit(solution)/shard_map/reduce_scatter | solution.py:87
  282.6 22.7 %copy-start.7 = (u32[32]{0:T(128)S(1)}, u32[32]{0:T(128)}, u32[]{:S(2)}) copy-start(u32[32]{0:T(128)} %constant.94) | copy-start | bytes 388
  282.6 156.4 %copy-start.6 = (f32[128,768]{1,0:T(8,128)S(1)}, f32[128,768]{1,0:T(8,128)}, u32[]{:S(2)}) copy-start(f32[128,768]{1,0:T(8,128)} %param.13) | copy-start | bytes 1179652
Sparse Core Ops, SparseCore 0:
  280.2 16.2 all-reduce.2
  305.4 133.5 reduce-scatter.1
